TPU v7x, 32 devices: a whole 2x2x4 slice. The times are simulated.
32 devices in a mesh: sec: 2 (over x), blk: 8 (over z, y), mp: 2 (over core).
Axes of the slice: x: 2, y: 2, z: 4, core: 2. Of those that a mesh axis runs over, the one named last changes fastest.
Arguments:
- image_pooled: bfloat16 [1536, 1536], P('blk', ('sec', 'mp')), may hold values from -4 to 4
- text_pooled: bfloat16 [1536, 2048], P('blk', ('sec', 'mp')), may hold values from -4 to 4
- image_proj: bfloat16 [1536, 1152], P(('sec', 'mp')), may hold values from -0.15625 to 0.15625
- text_proj: bfloat16 [2048, 1152], P(('sec', 'mp')), may hold values from -0.125 to 0.125
- natural_log_multiplier: float32 [1], replicated, may hold values from 1.4 to 2.3
- logit_bias: float32 [1], replicated, may hold values from -2 to -0.5
- match_cluster_labels: int32 [1536], P('blk'), may hold values from 0 to 1535
Outputs:
- pair_loss: float32 [2, 1536], P('sec', 'blk')
- image_grad: bfloat16 [1536, 1536], P('blk', ('sec', 'mp'))
- text_grad: bfloat16 [1536, 2048], P('blk', ('sec', 'mp'))
All inputs are finite; a program needn't handle non-finite values.
Results may differ from a plain program's by a relative error of at most 0.0065.
Values may be sent and summed in bfloat16 or wider, within the bound.
No kernel may reach another device: no remote copies, remote signals or barrier semaphores. Data moves between devices by JAX's collectives and lax.ppermute only.
A program may use at most 128 MiB of HBM per device.

v0:
```python
import jax
import jax.numpy as jnp
from jax import lax
from jax.sharding import PartitionSpec as P


def unit_rows(embedding):
    row_norm = jnp.sqrt(jnp.sum(embedding * embedding, axis=1, keepdims=True) + 1e-06)
    return (embedding / row_norm, row_norm)


def per_device(
    image_pooled,
    text_pooled,
    image_proj,
    text_proj,
    natural_log_multiplier,
    logit_bias,
    match_cluster_labels,
):
    part_image = jnp.dot(image_pooled, image_proj, preferred_element_type=jnp.float32)
    part_text = jnp.dot(text_pooled, text_proj, preferred_element_type=jnp.float32)
    stacked = jnp.stack([part_image, part_text])
    section = lax.axis_index("sec")
    both_sums = lax.psum(stacked, ("sec", "mp"))
    own_emb = lax.dynamic_index_in_dim(both_sums, section, 0, keepdims=False)
    other_emb = lax.dynamic_index_in_dim(both_sums, 1 - section, 0, keepdims=False)
    own_unit, own_norm = unit_rows(own_emb)
    resident_slice = own_unit.astype(jnp.bfloat16)
    other_unit, other_norm = unit_rows(other_emb)
    counterpart_slice = other_unit.astype(jnp.bfloat16)
    sharpness_factor = jnp.exp(natural_log_multiplier[0])
    shift_quantity = logit_bias[0]
    visit_rows = lax.all_gather(counterpart_slice, "blk", axis=0, tiled=True)
    visited_ids = lax.all_gather(match_cluster_labels, "blk", axis=0, tiled=True)
    agreement_scores_matrix = (
        sharpness_factor
        * lax.dot_general(
            resident_slice, visit_rows, (((1,), (1,)), ((), ())), preferred_element_type=jnp.float32
        )
        + shift_quantity
    )
    desired_polarity = jnp.where(
        match_cluster_labels[:, None] == visited_ids[None, :], 1.0, -1.0
    ).astype(jnp.float32)
    row_losses = jnp.sum(jax.nn.softplus(-desired_polarity * agreement_scores_matrix), axis=1)
    penalty_factor = (
        -sharpness_factor
        * desired_polarity
        * jax.nn.sigmoid(-desired_polarity * agreement_scores_matrix)
    ).astype(jnp.bfloat16)
    unit_grad = jnp.dot(penalty_factor, visit_rows, preferred_element_type=jnp.float32)
    unit_grad, row_losses = (unit_grad, row_losses)
    projection = jnp.sum(own_unit * unit_grad, axis=1, keepdims=True)
    own_demb = ((unit_grad - own_unit * projection) / own_norm).astype(jnp.bfloat16)
    both_grads = lax.all_gather(own_demb[None], "sec", axis=0, tiled=True)
    image_grad = lax.dot_general(
        both_grads[0], image_proj, (((1,), (1,)), ((), ())), preferred_element_type=jnp.float32
    ).astype(jnp.bfloat16)
    text_grad = lax.dot_general(
        both_grads[1], text_proj, (((1,), (1,)), ((), ())), preferred_element_type=jnp.float32
    ).astype(jnp.bfloat16)
    return (row_losses[None, :], image_grad, text_grad)


def solution(mesh):
    placed = (
        P("blk", ("sec", "mp")),
        P("blk", ("sec", "mp")),
        P(("sec", "mp"), None),
        P(("sec", "mp"), None),
        P(),
        P(),
        P("blk"),
    )
    return jax.shard_map(
        per_device,
        mesh=mesh,
        in_specs=placed,
        out_specs=(P("sec", "blk"), P("blk", ("sec", "mp")), P("blk", ("sec", "mp"))),
        check_vma=False,
    )
```

profile of v0, /device:TPU:0, one launch (start us, length us, event | category | flops | bytes accessed | tf_op | source)
XLA Modules:
  0.0 155.9 jit_solution(17890607806463199969)
XLA Ops:
  7.2 0.0 copy-start
  7.2 0.0 copy-start.4
  7.2 0.0 copy-start.2
  7.2 0.0 all-reduce.3.cloned.1.call-start
  7.2 1.2 copy-done
  8.4 1.4 convolution_bitcast_fusion
  9.8 0.0 copy-done.4
  9.8 0.0 copy-done.2
  9.8 0.4 convolution_bitcast_fusion.1
  10.2 1.3 pad_maximum_fusion
  11.6 0.0 all-reduce.3.cloned.1.call-update
  11.6 0.0 all-gather.3.cloned.1.call-start
  11.6 48.8 %all-reduce.3.cloned.1.call-done = f32[2,192,1152]{2,1,0:T(8,128)} async-done(((f32[2,192,1152]{2,1,0:T(8,128)}), f32[2,192,1152]{2,1,0:T(8,128)}) %all-reduce.3.cloned.1.call-update) | async-done | bytes 1769488 | tf_op jit(solution)/shard_map/psum | solution.py:25
  60.5 0.0 copy-start.1
  60.5 1.8 %fusion.7 = (f32[192]{0:T(256)S(1)}, f32[192]{0:T(256)S(1)}) fusion(f32[2,192,1152]{2,1,0:T(8,128)} %all-reduce.3.cloned.1.call-done, s32[]{:T(128)S(6)} %select_n.16, s32[]{:T(128)S(6)} %select_n.17), kind=kLoop, calls=%fused_computation.20 | loop fusion | flops 884352 | bytes 1771016 | tf_op jit(solution)/shard_map/reduce_sum | solution.py:8
  62.2 0.0 copy-start.7
  62.3 0.0 copy-start.5
  62.3 0.2 copy-done.1
  62.5 0.9 fusion.6
  63.4 0.0 all-gather.3.cloned.1.call-update
  64.7 0.0 copy-done.7
  64.8 0.6 dynamic-slice
  66.0 0.0 copy-done.5
  66.0 0.3 dynamic-update-slice
  66.3 12.1 %all-reduce = s32[1536]{0:T(1024)S(1)} all-reduce(s32[1536]{0:T(1024)S(1)} %dynamic-update-slice), channel_id=1, replica_groups=mesh['sec'=2,'blk'=8,'mp'=2] {'blk'}, use_global_device_ids=true, to_apply=%add | all-reduce | flops 1536 | bytes 12288
  78.4 50.5 %all-gather.3.cloned.1.call-done = bf16[1536,1152]{1,0:T(8,128)(2,1)} async-done(((bf16[192,1152]{1,0:T(8,128)(2,1)}), bf16[1536,1152]{1,0:T(8,128)(2,1)}) %all-gather.3.cloned.1.call-update) | async-done | bytes 3538960 | tf_op jit(solution)/shard_map/all_gather | solution.py:34
  128.9 0.0 copy-start.6
  128.9 4.7 %fusion.4 = (f32[192]{0:T(256)}, f32[192,1536]{1,0:T(8,128)S(1)}) fusion(f32[]{:T(128)} %bitcast.37, bf16[1536,1152]{1,0:T(8,128)(2,1)} %all-gather.3.cloned.1.call-done, f32[192]{0:T(256)S(1)} %add_sqrt_fusion.1, f32[2,192,1152]{2,1,0:T(8,128)S(1)} %copy-done.1, s32[]{:T(128)S(6)} %select_n.16, f32[]{:T(128)} %bitcast.1, s32[1536]{0:T(1024)S(1)} %all-reduce, ...), kind=kOutput, calls=%fused_computation.11 | convolution fusion | flops 683753280 | bytes 5614348 | tf_op jit(solution)/shard_map/dot_general | solution.py:38
  133.6 0.0 copy-done.6
  133.6 1.1 multiply_reduce_fusion
  134.7 0.2 divide_convert_fusion
  135.0 0.0 copy-start.3
  135.0 11.7 %all-gather = bf16[384,1152]{1,0:T(8,128)(2,1)S(1)} all-gather(bf16[192,1152]{1,0:T(8,128)(2,1)S(1)} %divide_convert_fusion), channel_id=2, replica_groups=mesh['sec'=2,'blk'=8,'mp'=2] {'sec'}, dimensions={0}, use_global_device_ids=true | all-gather | bytes 1327104 | tf_op jit(solution)/shard_map/all_gather | solution.py:56
  146.7 0.0 copy-done.3
  146.7 1.1 convolution_convert_fusion.1
  147.8 1.2 convolution_convert_fusion
  (3 shorter events, 0.0 us)
Async XLA Ops:
  7.2 1.3 copy-start
  7.2 2.6 %copy-start.4 = (bf16[192,384]{1,0:T(8,128)(2,1)S(1)}, bf16[192,384]{1,0:T(8,128)(2,1)}, u32[]{:S(2)}) copy-start(bf16[192,384]{1,0:T(8,128)(2,1)} %param.7) | copy-start | bytes 442372
  7.2 2.6 %copy-start.2 = (bf16[384,1152]{1,0:T(8,128)(2,1)S(1)}, bf16[384,1152]{1,0:T(8,128)(2,1)}, u32[]{:S(2)}) copy-start(bf16[384,1152]{1,0:T(8,128)(2,1)} %param.9) | copy-start | bytes 2654212
  7.2 53.3 %all-reduce.3.cloned.1.call-start = ((), (), s32[]{:S(2)}) async-start(), calls=%async_computation | async-start | bytes 3538944 | tf_op jit(solution)/shard_map/psum | solution.py:25
  11.6 117.3 %all-gather.3.cloned.1.call-start = ((), (), s32[]{:S(2)}) async-start(), calls=%async_computation.1 | async-start | bytes 3981312 | tf_op jit(solution)/shard_map/all_gather | solution.py:34
  60.5 2.0 %copy-start.1 = (f32[2,192,1152]{2,1,0:T(8,128)S(1)}, f32[2,192,1152]{2,1,0:T(8,128)}, u32[]{:S(2)}) copy-start(f32[2,192,1152]{2,1,0:T(8,128)} %all-reduce.3.cloned.1.call-done) | copy-start | bytes 5308420
  62.2 2.5 %copy-start.7 = (u32[32]{0:T(128)S(1)}, u32[32]{0:T(128)}, u32[]{:S(2)}) copy-start(u32[32]{0:T(128)} %constant.31) | copy-start | bytes 388
  62.3 3.8 %copy-start.5 = (s32[192]{0:T(256)S(1)}, s32[192]{0:T(256)}, u32[]{:S(2)}) copy-start(s32[192]{0:T(256)} %param.13) | copy-start | bytes 2308
  128.9 4.7 %copy-start.6 = (bf16[1536,1152]{1,0:T(8,128)(2,1)S(1)}, bf16[1536,1152]{1,0:T(8,128)(2,1)}, u32[]{:S(2)}) copy-start(bf16[1536,1152]{1,0:T(8,128)(2,1)} %all-gather.3.cloned.1.call-done) | copy-start | bytes 10616836
  135.0 11.8 %copy-start.3 = (bf16[384,1152]{1,0:T(8,128)(2,1)S(1)}, bf16[384,1152]{1,0:T(8,128)(2,1)}, u32[]{:S(2)}) copy-start(bf16[384,1152]{1,0:T(8,128)(2,1)} %param.9) | copy-start | bytes 2654212
Sparse Core Ops, SparseCore 0:
  11.7 48.7 all-reduce.2
  63.5 65.3 all-gather.2
where the time goes:
time: 156 us
  waiting for transfers between devices  99.4 us (64%)
  blocking collectives  23.8 us (15%)
  between operations  16.2 us (10%)
  matrix products  9.9 us (6%)
  other arithmetic  4.2 us (3%)
  local copies, waits for them, and re-layouts  2.31 us (1%)
    all_gather x1, waiting for transfers between devices, per_device(): visit_rows = lax.all_gather(counterpart_slice, 'blk', axis=0, tiled=True)  50.5 us
    psum x1, waiting for transfers between devices, per_device(): both_sums = lax.psum(stacked, ('sec', 'mp'))  48.8 us
    unnamed x1, blocking collectives  12.1 us
    all_gather x1, blocking collectives, per_device(): both_grads = lax.all_gather(own_demb[None], 'sec', axis=0, tiled=True)  11.7 us
    dot_general x1, matrix products, per_device(): lax.dot_general(resident_slice, visit_rows, (((1,), (1,)), ((), ())), pre...  4.68 us
  transfers between devices with their start and end apart: 2, of which 2 were waited for; matrix products, arithmetic and copies ran while one was open for 1% of the time, Pallas kernels for 0%

commit v1 on v0

--- a/solution.py
+++ b/solution.py
@@ -22,7 +22,7 @@
     part_text = jnp.dot(text_pooled, text_proj, preferred_element_type=jnp.float32)
     stacked = jnp.stack([part_image, part_text])
     section = lax.axis_index("sec")
-    both_sums = lax.psum(stacked, ("sec", "mp"))
+    both_sums = jnp.sum(lax.all_gather(stacked, ("sec", "mp")), axis=0)
     own_emb = lax.dynamic_index_in_dim(both_sums, section, 0, keepdims=False)
     other_emb = lax.dynamic_index_in_dim(both_sums, 1 - section, 0, keepdims=False)
     own_unit, own_norm = unit_rows(own_emb)

time: 156 us -> 163 us (1.045)
  waiting for transfers between devices: 99.4 us -> 104 us
  other arithmetic: 4.2 us -> 6.33 us
    all_gather x0 -> x1, waiting for transfers between devices: none -> 53.6 us  [per_device(): both_sums = jnp.sum(lax.all_gather(stacked, ('sec', 'mp')), axis=0)]
    psum x1 -> x0, waiting for transfers between devices: 48.8 us -> none  [per_device(): both_sums = lax.psum(stacked, ('sec', 'mp'))]
    reduce_sum x0 -> x1, other arithmetic: none -> 3.58 us  [per_device(): both_sums = jnp.sum(lax.all_gather(stacked, ('sec', 'mp')), axis=0)]
where the time goes in v1:
time: 163 us
  waiting for transfers between devices  104 us (64%)
  blocking collectives  23.8 us (15%)
  between operations  16.2 us (10%)
  matrix products  9.9 us (6%)
  other arithmetic  6.33 us (4%)
  local copies, waits for them, and re-layouts  2.1 us (1%)
    all_gather x1, waiting for transfers between devices, per_device(): both_sums = jnp.sum(lax.all_gather(stacked, ('sec', 'mp')), axis=0)  53.6 us
    all_gather x1, waiting for transfers between devices, per_device(): visit_rows = lax.all_gather(counterpart_slice, 'blk', axis=0, tiled=True)  50.5 us
    unnamed x1, blocking collectives  12.1 us
    all_gather x1, blocking collectives, per_device(): both_grads = lax.all_gather(own_demb[None], 'sec', axis=0, tiled=True)  11.7 us
    dot_general x1, matrix products, per_device(): lax.dot_general(resident_slice, visit_rows, (((1,), (1,)), ((), ())), pre...  4.68 us
    reduce_sum x1, other arithmetic, per_device(): both_sums = jnp.sum(lax.all_gather(stacked, ('sec', 'mp')), axis=0)  3.58 us
  transfers between devices with their start and end apart: 2, of which 2 were waited for; matrix products, arithmetic and copies ran while one was open for 1% of the time, Pallas kernels for 0%

profile of v1, /device:TPU:0, one launch (start us, length us, event | category | flops | bytes accessed | tf_op | source)
XLA Modules:
  0.0 162.5 jit_solution(6707643929582511665)
XLA Ops:
  7.2 0.0 copy-start
  7.2 0.0 copy-start.3
  7.2 0.0 copy-start.1
  7.2 0.0 all-gather.7.cloned.1.call-start
  7.2 1.2 copy-done
  8.4 1.4 convolution_bitcast_fusion
  9.8 0.0 copy-done.3
  9.8 0.0 copy-done.1
  9.8 0.4 convolution_bitcast_fusion.1
  10.2 1.4 pad_maximum_fusion
  11.6 0.0 all-gather.7.cloned.1.call-update
  11.7 0.0 all-gather.5.cloned.1.call-start
  11.7 53.6 %all-gather.7.cloned.1.call-done = f32[8,192,1152]{2,1,0:T(8,128)} async-done(((f32[2,192,1152]{2,1,0:T(8,128)}), f32[8,192,1152]{2,1,0:T(8,128)}) %all-gather.7.cloned.1.call-update) | async-done | bytes 7077904 | tf_op jit(solution)/shard_map/all_gather | solution.py:25
  65.4 3.6 %reduce_sum.45 = f32[2,192,1152]{2,1,0:T(8,128)S(1)} reduce(f32[4,2,192,1152]{3,2,1,0:T(8,128)} %bitcast.39, f32[]{:T(128)} %constant.12.clone.1), dimensions={0}, to_apply=%region_0.0 | reduce | flops 1327104 | bytes 8847364 | tf_op jit(solution)/shard_map/reduce_sum | solution.py:25
  69.0 0.2 fusion.7
  69.2 0.0 copy-start.6
  69.2 0.0 copy-start.4
  69.2 0.9 fusion.6
  70.1 0.0 all-gather.5.cloned.1.call-update
  71.4 0.0 copy-done.6
  71.5 0.6 dynamic-slice
  72.7 0.0 copy-done.4
  72.7 0.3 dynamic-update-slice
  73.0 12.1 %all-reduce = s32[1536]{0:T(1024)S(1)} all-reduce(s32[1536]{0:T(1024)S(1)} %dynamic-update-slice), channel_id=1, replica_groups=mesh['sec'=2,'blk'=8,'mp'=2] {'blk'}, use_global_device_ids=true, to_apply=%add | all-reduce | flops 1536 | bytes 12288
  85.1 50.5 %all-gather.5.cloned.1.call-done = bf16[1536,1152]{1,0:T(8,128)(2,1)} async-done(((bf16[192,1152]{1,0:T(8,128)(2,1)}), bf16[1536,1152]{1,0:T(8,128)(2,1)}) %all-gather.5.cloned.1.call-update) | async-done | bytes 3538960 | tf_op jit(solution)/shard_map/all_gather | solution.py:34
  135.6 0.0 copy-start.5
  135.6 4.7 %fusion.4 = (f32[192]{0:T(256)}, f32[192,1536]{1,0:T(8,128)S(1)}) fusion(f32[]{:T(128)} %bitcast.38, bf16[1536,1152]{1,0:T(8,128)(2,1)} %all-gather.5.cloned.1.call-done, f32[192]{0:T(256)S(1)} %add_sqrt_fusion.1, f32[2,192,1152]{2,1,0:T(8,128)S(1)} %reduce_sum.45, s32[]{:T(128)S(6)} %select_n.16, f32[]{:T(128)} %bitcast.1, s32[1536]{0:T(1024)S(1)} %all-reduce, ...), kind=kOutput, calls=%fused_computation.11 | convolution fusion | flops 683753280 | bytes 5614348 | tf_op jit(solution)/shard_map/dot_general | solution.py:38
  140.2 0.0 copy-done.5
  140.2 1.1 multiply_reduce_fusion
  141.4 0.2 divide_convert_fusion
  141.6 0.0 copy-start.2
  141.6 11.7 %all-gather.1 = bf16[384,1152]{1,0:T(8,128)(2,1)S(1)} all-gather(bf16[192,1152]{1,0:T(8,128)(2,1)S(1)} %divide_convert_fusion), channel_id=3, replica_groups=mesh['sec'=2,'blk'=8,'mp'=2] {'sec'}, dimensions={0}, use_global_device_ids=true | all-gather | bytes 1327104 | tf_op jit(solution)/shard_map/all_gather | solution.py:56
  153.4 0.0 copy-done.2
  153.4 1.1 convolution_convert_fusion.1
  154.5 1.2 convolution_convert_fusion
  (3 shorter events, 0.0 us)
Async XLA Ops:
  7.2 1.3 copy-start
  7.2 2.6 %copy-start.3 = (bf16[192,384]{1,0:T(8,128)(2,1)S(1)}, bf16[192,384]{1,0:T(8,128)(2,1)}, u32[]{:S(2)}) copy-start(bf16[192,384]{1,0:T(8,128)(2,1)} %param.7) | copy-start | bytes 442372
  7.2 2.6 %copy-start.1 = (bf16[384,1152]{1,0:T(8,128)(2,1)S(1)}, bf16[384,1152]{1,0:T(8,128)(2,1)}, u32[]{:S(2)}) copy-start(bf16[384,1152]{1,0:T(8,128)(2,1)} %param.9) | copy-start | bytes 2654212
  7.2 58.2 %all-gather.7.cloned.1.call-start = ((), (), s32[]{:S(2)}) async-start(), calls=%async_computation.1 | async-start | bytes 8847360 | tf_op jit(solution)/shard_map/all_gather | solution.py:25
  11.7 123.9 %all-gather.5.cloned.1.call-start = ((), (), s32[]{:S(2)}) async-start(), calls=%async_computation | async-start | bytes 3981312 | tf_op jit(solution)/shard_map/all_gather | solution.py:34
  69.2 2.3 %copy-start.6 = (u32[32]{0:T(128)S(1)}, u32[32]{0:T(128)}, u32[]{:S(2)}) copy-start(u32[32]{0:T(128)} %constant.31) | copy-start | bytes 388
  69.2 3.5 %copy-start.4 = (s32[192]{0:T(256)S(1)}, s32[192]{0:T(256)}, u32[]{:S(2)}) copy-start(s32[192]{0:T(256)} %param.13) | copy-start | bytes 2308
  135.6 4.7 %copy-start.5 = (bf16[1536,1152]{1,0:T(8,128)(2,1)S(1)}, bf16[1536,1152]{1,0:T(8,128)(2,1)}, u32[]{:S(2)}) copy-start(bf16[1536,1152]{1,0:T(8,128)(2,1)} %all-gather.5.cloned.1.call-done) | copy-start | bytes 10616836
  141.6 11.8 %copy-start.2 = (bf16[384,1152]{1,0:T(8,128)(2,1)S(1)}, bf16[384,1152]{1,0:T(8,128)(2,1)}, u32[]{:S(2)}) copy-start(bf16[384,1152]{1,0:T(8,128)(2,1)} %param.9) | copy-start | bytes 2654212
Sparse Core Ops, SparseCore 0:
  11.8 53.5 all-gather.6
  70.2 65.2 all-gather.4
